TPU v7x, 32 devices: a whole 2x2x4 slice. The times are simulated.
32 devices in a mesh: cell: 8 (over z, x), patch: 4 (over y, core).
Axes of the slice: x: 2, y: 2, z: 4, core: 2. Of those that a mesh axis runs over, the one named last changes fastest.
Arguments:
- right_side: float32 [256, 3, 2112], P('cell', None, 'patch'), may hold values from -45 to 45
- analysis: float32 [2112, 1089], P('patch'), may hold values from -0.125 to 0.125
- spectral: float32 [256, 1089], P('cell'), may hold values from 0.1 to 10
- near_kernel: float32 [2112, 2112], P(None, 'patch'), may hold values from -0.125 to 0.125
- near_send: int32 [8, 8, 8], P('cell'), may hold values from 0 to 31, as said below
- near_target: int32 [8, 8, 8], P('cell'), may hold values from -1 to 31, as said below
- near_strength: float32 [8, 8, 8], P('cell'), may hold values from 0.2 to 1
Outputs:
- solution: float32 [256, 3, 2112], P('cell', None, 'patch')
- relative_residual: float32 [], replicated
Inputs may be any that keep to these rules, and one draw needn't show every extreme that they name: `near_send`: each entry names one of the 32 cells of the sending group. Slot s of near_send[d, q] pairs with slot s of near_target[q, d]. Live slots come first. From group d to a group q at index distance at most one modulo 8 (d itself included) at most 8 slots are live, to any other group at most 2; both bounds are reached in every draw.
All inputs are finite; a program needn't handle non-finite values.
Results may differ from a plain program's by a relative error of at most 0.0003.
Values sent between devices are 32-bit elements; how exact they have to be, the bound alone decides.
A program may use at most 128 MiB of HBM per device.

v0:
```python
import functools

import jax
import jax.numpy as jnp
from jax import lax
from jax.experimental import pallas as pl
from jax.experimental.pallas import tpu as pltpu
from jax.sharding import PartitionSpec as P

ITERS = 8
FAR_CAP = 2
LANES = 128
MSG = 16
F32 = jnp.float32
BF16 = jnp.bfloat16
MESH = pl.DeviceIdType.MESH


def round_up(value, unit):
    return -(-value // unit) * unit


def split(x):
    hi = x.astype(BF16)
    return hi, (x - hi.astype(F32)).astype(BF16)


def halves(x):
    return x[:, :LANES] + x[:, LANES:]


def dot(a, b):
    return jnp.dot(a, b, preferred_element_type=F32)


def dot_nt(a, b):
    return lax.dot_general(a, b, (((1,), (1,)), ((), ())), preferred_element_type=F32)


def dot_tn(a, b):
    return lax.dot_general(a, b, (((0,), (0,)), ((), ())), preferred_element_type=F32)


def blocks_of(groups, near_rows, far_rows):
    out, at = {}, 0
    for d in sorted(range(groups), key=lambda d: (min(d, groups - d) > 1, d)):
        rows = near_rows if min(d, groups - d) <= 1 else far_rows
        out[d] = (at, rows)
        at += rows
    return out, at


def packed_rows(rows):
    return round_up(rows * 3 // 4, 8)


def pack(dst, x, lanes):
    idle = LANES - lanes
    main = dst.shape[0]
    tail = x.shape[0] - main
    lane = lax.broadcasted_iota(jnp.int32, (1, LANES), 1)
    dst[...] = x[:main]
    for i in range(lanes // idle):
        rows = slice(i * tail, (i + 1) * tail)
        moved = pltpu.roll(x[main:], lanes - idle * i, 1)
        dst[rows, :] = jnp.where(lane >= lanes, moved, x[rows])


def unpack(src, total, lanes):
    idle = LANES - lanes
    main = src.shape[0]
    tail = total - main
    lane = lax.broadcasted_iota(jnp.int32, (1, LANES), 1)
    end = jnp.zeros((tail, LANES), F32)
    for i in range(lanes // idle):
        moved = pltpu.roll(src[i * tail : (i + 1) * tail], (idle * i - lanes) % LANES, 1)
        end = jnp.where((lane >= idle * i) & (lane < idle * (i + 1)), moved, end)
    return jnp.concatenate((jnp.where(lane < lanes, src, 0.0), end), 0)


def pieces_of(rows):
    return next(n for n in (1,) if rows // 8 % n == 0)


def tile_rows(total, unit, most):
    best = unit
    for rows in range(unit, most + 1, unit):
        if total % rows == 0:
            best = rows
    return best


def kernel(
    groups, patches, lanes, blocks,
    u0, kernel_t, amine, aother, bmat, spec, sel, mix,
    out, res,
    image, packed, basis, vs, cs, pair, khi, klo, ahi, alo, bhi, blo, part_out, part_in, half_out, half_in,
    sendrows, recvrows, msg1, msg2, hess, hrows,
    ag_send, ag_recv, fw_send, fw_recv, s1_send, s1_recv, s2_send, s2_recv, a2_send, a2_recv,
    cf_send, cf_recv, sw_send, sw_recv,
):
    points = u0.shape[0]
    total = basis.shape[1]
    half = spec.shape[1]
    main = packed.shape[2]
    pieces = pieces_of(main)
    chunk = main // pieces
    width = 2 * points
    g = lax.axis_index("cell")
    p = lax.axis_index("patch")
    core = lax.rem(p, 2)
    chip = p // 2
    sib = p + 1 - 2 * core
    chips = patches // 2

    msg1[...] = jnp.zeros_like(msg1)
    barrier = pltpu.get_barrier_semaphore()
    for d in range(1, groups):
        pl.semaphore_signal(barrier, inc=1, device_id=(lax.rem(g + d, groups), p), device_id_type=MESH)
    for d in range(1, patches):
        pl.semaphore_signal(barrier, inc=1, device_id=(g, lax.rem(p + d, patches)), device_id_type=MESH)

    hess[...] = jnp.zeros_like(hess)
    mine = pl.ds(pl.multiple_of(p * points, 8), points)

    image[mine, :] = u0[...]
    pl.semaphore_wait(barrier, groups + patches - 2)

    swap = pltpu.make_async_remote_copy(
        src_ref=aother, dst_ref=pair.at[core],
        send_sem=sw_send.at[1], recv_sem=sw_recv.at[1],
        device_id=(g, sib), device_id_type=MESH,
    )
    swap.start()
    for c in range(chips):
        khi[c], klo[c] = split(kernel_t[:, c * width : (c + 1) * width])
    for c in range(2):
        bhi[c], blo[c] = split(bmat[:, c * half : (c + 1) * half])
    pair[core] = amine[...]
    swap.wait()
    ahi[...], alo[...] = split(pair[...].reshape(width, half).T)

    def dots(slot, count):
        def one(i, carry):
            msg1[slot, p, pl.ds(i, 1), :] = jnp.sum(basis[i, mine, :] * image[mine, :], axis=0, keepdims=True)
            return carry

        lax.fori_loop(0, count, one, 0)
        msg1[slot, p, ITERS : ITERS + 1, :] = jnp.sum(image[mine, :] * image[mine, :], axis=0, keepdims=True)

    def stage1(slot):
        return [
            pltpu.make_async_remote_copy(
                src_ref=msg1.at[slot, p], dst_ref=msg1.at[slot, p],
                send_sem=s1_send.at[slot, d], recv_sem=s1_recv.at[slot, d],
                device_id=(g, lax.rem(p + d, patches)), device_id_type=MESH,
            )
            for d in range(1, patches)
        ]

    def stage2(slot):
        return [
            pltpu.make_async_remote_copy(
                src_ref=msg2.at[slot, g], dst_ref=msg2.at[slot, g],
                send_sem=s2_send.at[slot, d], recv_sem=s2_recv.at[slot, d],
                device_id=(lax.rem(g + d, groups), p), device_id_type=MESH,
            )
            for d in range(1, groups)
        ]

    def reduce_sums(slot, first):
        for c in first:
            c.wait()
        local = msg1[slot, 0]
        for q in range(1, patches):
            local = local + msg1[slot, q]
        msg2[slot, g] = local
        second = stage2(slot)
        for c in second:
            c.start()
        for c in second:
            c.wait()
        whole = msg2[slot, 0]
        for q in range(1, groups):
            whole = whole + msg2[slot, q]
        return jnp.sum(whole, axis=1, keepdims=True)

    row_ids = lax.broadcasted_iota(jnp.int32, (MSG, 1), 0)
    lane_ids = lax.broadcasted_iota(jnp.int32, (1, LANES), 1)

    def record(step, sums):
        squared = sums[ITERS : ITERS + 1, :]
        h = jnp.where(row_ids < ITERS, sums, 0.0)
        length = jnp.sqrt(squared - jnp.sum(h * h, axis=0, keepdims=True))
        column = jnp.where(row_ids == step, length, h)
        lane = lax.rem(step + ITERS, ITERS + 1)
        hess[...] = jnp.where(lane_ids == lane, column, hess[...])
        return h, length

    vrows = tile_rows(width, 16, 192)

    def body(step, carry):
        slot = lax.rem(step, 2)
        pack(packed.at[slot, p], image[mine, :], lanes)
        own = pltpu.make_async_remote_copy(
            src_ref=packed.at[slot, p], dst_ref=packed.at[slot, p],
            send_sem=ag_send.at[slot, 0, 0], recv_sem=ag_recv.at[slot, 0, 0],
            device_id=(g, sib), device_id_type=MESH,
        )
        cross, forward = [], []
        for n in range(pieces):
            rows = pl.ds(n * chunk, chunk)
            for k in range(1, chips):
                cross.append(pltpu.make_async_remote_copy(
                    src_ref=packed.at[slot, p, rows], dst_ref=packed.at[slot, p, rows],
                    send_sem=ag_send.at[slot, k, n], recv_sem=ag_recv.at[slot, k, n],
                    device_id=(g, lax.rem(p + 2 * k, patches)), device_id_type=MESH,
                ))
                src = lax.rem(p + patches - 2 * k, patches)
                forward.append(pltpu.make_async_remote_copy(
                    src_ref=packed.at[slot, src, rows], dst_ref=packed.at[slot, src, rows],
                    send_sem=fw_send.at[slot, k, n], recv_sem=fw_recv.at[slot, k, n],
                    device_id=(g, sib), device_id_type=MESH,
                ))
        dots(slot, step)
        first = stage1(slot)
        for c in first:
            c.start()
        for c in cross:
            c.start()
        own.start()
        h, length = record(step, reduce_sums(slot, first))
        scale = jnp.broadcast_to(1.0 / length, (1, LANES))
        hrows[...] = jnp.broadcast_to(h, (MSG, LANES))

        def update(which):
            @pl.loop(0, width // vrows)
            def _(t):
                at = pl.multiple_of(t * vrows, 16)
                rows = pl.ds(pl.multiple_of(which * width + at, 16), vrows)
                v = lax.fori_loop(
                    0, step,
                    lambda i, v: v - hrows[pl.ds(i, 1), :] * basis[i, rows, :],
                    image[rows, :],
                )
                v = v * scale
                basis[step, rows, :] = v
                hi, lo = split(v)
                vs[rows, :LANES] = hi
                vs[rows, LANES:] = lo

        def wide(which):
            return vs[pl.ds(pl.multiple_of(which * width, 16), width), :]

        def place(who):
            rows = pl.ds(pl.multiple_of(who * points, 8), points)
            image[rows, :] = unpack(packed[slot, who], points, lanes)

        own.wait()
        place(sib)
        update(chip)
        for c, f in zip(cross, forward):
            c.wait()
            f.start()
        pack(part_out, halves(dot(ahi[...], wide(chip)) + dot(alo[...], wide(chip))), lanes)
        partials = [
            pltpu.make_async_remote_copy(
                src_ref=part_out, dst_ref=part_in.at[k - 1],
                send_sem=cf_send.at[k], recv_sem=cf_recv.at[k],
                device_id=(g, lax.rem(p + 2 * k, patches)), device_id_type=MESH,
            )
            for k in range(1, chips)
        ]
        for c in partials:
            c.start()
        acc = dot(khi[chip], wide(chip)) + dot(klo[chip], wide(chip))
        for f in forward:
            f.wait()
        for k in range(1, chips):
            other = lax.rem(chip + chips - k, chips)
            place(2 * other)
            place(2 * other + 1)
            update(other)
            acc = acc + (dot(khi[other], wide(other)) + dot(klo[other], wide(other)))
        whi, wlo = split(halves(acc))
        sendrows[...] = dot_nt(sel[...], whi) + dot_nt(sel[...], wlo)
        sends = []
        for d in sorted(range(1, groups), key=lambda d: min(d, groups - d) > 1):
            at, rows = blocks[d]
            sends.append(pltpu.make_async_remote_copy(
                src_ref=sendrows.at[pl.ds(at, rows)], dst_ref=recvrows.at[pl.ds(at, rows)],
                send_sem=a2_send.at[d], recv_sem=a2_recv.at[d],
                device_id=(lax.rem(g + d, groups), p), device_id_type=MESH,
            ))
        for c in sends:
            c.start()
        recvrows[: blocks[0][1], :] = sendrows[: blocks[0][1], :]

        coef = part_out[...]
        for k, c in enumerate(partials, 1):
            c.wait()
            coef = coef + part_in[k - 1]
        half_out[...] = coef
        exchange = pltpu.make_async_remote_copy(
            src_ref=half_out, dst_ref=half_in,
            send_sem=sw_send.at[0], recv_sem=sw_recv.at[0],
            device_id=(g, sib), device_id_type=MESH,
        )
        exchange.start()

        def self_half(which, values):
            hi, lo = split(values)
            cs[:, :LANES] = hi
            cs[:, LANES:] = lo
            return halves(dot(bhi[which], cs[...]) + dot(blo[which], cs[...]))

        new = basis[step, mine, :] + self_half(core, unpack(coef, half, lanes) * spec[core])
        exchange.wait()
        new = new + self_half(1 - core, unpack(half_in[...], half, lanes) * spec[1 - core])
        for c in sends:
            c.wait()
        rhi, rlo = split(recvrows[...])
        mixes = jnp.concatenate(split(mix[...]), 1)
        new = new + halves(dot_tn(rhi, mixes) + dot_tn(rlo, mixes))
        image[mine, :] = new
        return carry

    lax.fori_loop(0, ITERS, body, 0)

    slot = ITERS % 2
    dots(slot, ITERS)
    first = stage1(slot)
    for c in first:
        c.start()
    record(ITERS, reduce_sums(slot, first))

    work = hess[...]
    beta = work[0:1, ITERS : ITERS + 1]
    rows = []
    for k in range(ITERS):
        col = work[:, k : k + 1]
        prods = jnp.sum(col * work, axis=0, keepdims=True)
        row = prods / prods[:, k : k + 1]
        rows.append(jnp.where(lane_ids >= k, row, 0.0))
        work = work - jnp.where(lane_ids >= k, col * row, 0.0)
    y = jnp.where(lane_ids == ITERS, -1.0, jnp.zeros((1, LANES), F32))
    for k in reversed(range(ITERS)):
        value = -jnp.sum(rows[k] * y, axis=1, keepdims=True)
        y = jnp.where(lane_ids == k, value, y)
    answer = y[:, 0:1] * basis[0, mine, :]
    for k in range(1, ITERS):
        answer = answer + y[:, k : k + 1] * basis[k, mine, :]
    out[...] = answer
    left = work[:, ITERS : ITERS + 1]
    norm = jnp.sqrt(jnp.sum(left * left, axis=0, keepdims=True)) / beta
    res[...] = jnp.broadcast_to(norm, res.shape)


def per_device(groups, patches, right_side, analysis, spectral, near_kernel, near_send, near_target, near_strength):
    cells, comps, points = right_side.shape
    total = near_kernel.shape[0]
    modes = analysis.shape[1]
    lanes = cells * comps
    cap = near_send.shape[-1]
    low = modes // 2
    half = round_up(modes - low, 16)
    pad = LANES - lanes
    near_rows, far_rows = cap * comps, round_up(FAR_CAP * comps, 8)
    blocks, total_rows = blocks_of(groups, near_rows, far_rows)
    g = lax.axis_index("cell")
    core = lax.rem(lax.axis_index("patch"), 2)

    u0 = jnp.pad(right_side.reshape(lanes, points).T, ((0, 0), (0, pad)))
    kernel_t = near_kernel.T

    def two_halves(x, axis):
        def padded(piece):
            pads = [(0, 0)] * x.ndim
            pads[axis] = (0, half - piece.shape[axis])
            return jnp.pad(piece, pads)

        return (
            padded(lax.slice_in_dim(x, 0, low, axis=axis)),
            padded(lax.slice_in_dim(x, low, modes, axis=axis)),
        )

    first, second = two_halves(analysis, 1)
    bmat = jnp.concatenate((first, second), 1)
    amine = jnp.where(core == 0, first, second)
    aother = jnp.where(core == 0, second, first)
    spec_first, spec_second = two_halves(spectral, 1)
    spec = jnp.stack((spec_first.T, spec_second.T))
    spec = jnp.pad(jnp.repeat(spec, comps, axis=2), ((0, 0), (0, 0), (0, pad)))

    def slot_rows(x, fill):
        close = jnp.concatenate((x[:2], x[groups - 1 :]), 0)
        far = x[2 : groups - 1, :FAR_CAP]
        close = jnp.broadcast_to(close[:, :, None], close.shape + (comps,)).reshape(-1)
        far = jnp.broadcast_to(far[:, :, None], far.shape + (comps,)).reshape(-1, FAR_CAP * comps)
        far = jnp.pad(far, ((0, 0), (0, far_rows - FAR_CAP * comps)), constant_values=fill).reshape(-1)
        return jnp.concatenate((close, far))[:, None]

    def ahead(x):
        return lax.dynamic_slice_in_dim(jnp.concatenate((x, x), 0), g, groups, 0)

    def behind(x):
        return lax.dynamic_slice_in_dim(jnp.concatenate((x, x), 0), g + 1, groups, 0)[::-1]

    row_comp = jnp.concatenate((
        jnp.tile(jnp.arange(comps), 3 * cap),
        jnp.tile(jnp.pad(jnp.tile(jnp.arange(comps), FAR_CAP), (0, far_rows - FAR_CAP * comps), constant_values=-1), groups - 3),
    ))[:, None]
    lane = jnp.arange(LANES)[None, :]
    same = (row_comp == lane % comps) & (lane < lanes)
    sel = (same & (slot_rows(ahead(near_send[0]), -1) == lane // comps)).astype(BF16)
    hit = same & (slot_rows(behind(near_target[0]), -1) == lane // comps)
    mix = jnp.where(hit, slot_rows(behind(near_strength[0]), 0.0), 0.0)

    vmem = pl.BlockSpec(memory_space=pltpu.VMEM)
    dma = pltpu.SemaphoreType.DMA
    chips = max(patches // 2, 1)
    main = packed_rows(points)
    pieces = pieces_of(main)
    answer, residual = pl.pallas_call(
        functools.partial(kernel, groups, patches, lanes, blocks),
        out_shape=(
            jax.ShapeDtypeStruct((points, LANES), F32),
            jax.ShapeDtypeStruct((8, LANES), F32),
        ),
        in_specs=[vmem] * 8,
        out_specs=(vmem, vmem),
        scratch_shapes=[
            pltpu.VMEM((total, LANES), F32),
            pltpu.VMEM((2, patches, main, LANES), F32),
            pltpu.VMEM((ITERS, total, LANES), F32),
            pltpu.VMEM((total, 2 * LANES), BF16),
            pltpu.VMEM((half, 2 * LANES), BF16),
            pltpu.VMEM((2, points, half), F32),
            pltpu.VMEM((chips, points, 2 * points), BF16),
            pltpu.VMEM((chips, points, 2 * points), BF16),
            pltpu.VMEM((half, 2 * points), BF16),
            pltpu.VMEM((half, 2 * points), BF16),
            pltpu.VMEM((2, points, half), BF16),
            pltpu.VMEM((2, points, half), BF16),
            pltpu.VMEM((packed_rows(half), LANES), F32),
            pltpu.VMEM((max(chips - 1, 1), packed_rows(half), LANES), F32),
            pltpu.VMEM((packed_rows(half), LANES), F32),
            pltpu.VMEM((packed_rows(half), LANES), F32),
            pltpu.VMEM((total_rows, points), F32),
            pltpu.VMEM((total_rows, points), F32),
            pltpu.VMEM((2, patches, MSG, LANES), F32),
            pltpu.VMEM((2, groups, MSG, LANES), F32),
            pltpu.VMEM((MSG, LANES), F32),
            pltpu.VMEM((MSG, LANES), F32),
            dma((2, chips, pieces)), dma((2, chips, pieces)), dma((2, chips, pieces)), dma((2, chips, pieces)),
            dma((2, patches)), dma((2, patches)), dma((2, groups)), dma((2, groups)),
            dma((groups,)), dma((groups,)),
            dma((chips,)), dma((chips,)), dma((2,)), dma((2,)),
        ],
        compiler_params=pltpu.CompilerParams(
            collective_id=0, has_side_effects=True, vmem_limit_bytes=60 * 1024 * 1024
        ),
        name="gmres",
    )(u0, kernel_t, amine, aother, bmat, spec, sel, mix)
    solution = answer[:, :lanes].T.reshape(cells, comps, points)
    return solution, residual[0, 0]


def solution(mesh):
    placed = (
        P("cell", None, "patch"),
        P("patch", None),
        P("cell", None),
        P(None, "patch"),
        P("cell", None, None),
        P("cell", None, None),
        P("cell", None, None),
    )
    return jax.shard_map(
        functools.partial(per_device, mesh.shape["cell"], mesh.shape["patch"]),
        mesh=mesh,
        in_specs=placed,
        out_specs=(P("cell", None, "patch"), P()),
        check_vma=False,
    )
```

profile of v0, /device:TPU:0, one launch (start us, length us, event | category | flops | bytes accessed | tf_op | source)
XLA Modules:
  0.0 201.9 jit_solution(2301552790451413250)
XLA Ops:
  0.6 0.8 fusion.1
  2.0 0.8 fusion
  3.4 0.8 fusion.2
  4.7 0.1 tile.13
  5.1 0.7 and_select_fusion.mix
  5.8 0.7 and_convert_fusion.sel
  6.6 1.9 slice.62
  8.5 0.2 copy-done
  8.6 1.9 broadcast_select_fusion
  10.5 1.9 pad_maximum_fusion.bmat
  12.5 0.1 copy.20
  12.7 0.1 broadcast_in_dim.22
  12.8 0.3 copy.21
  13.1 0.9 pad.44.spec
  13.9 0.2 copy.18
  14.1 0.1 reshape.91
  14.3 0.1 copy.19
  14.4 0.7 pad.39.u0
  15.1 183.6 %gmres.1 = (f32[528,128]{1,0:T(8,128)}, f32[8,128]{1,0:T(8,128)}) custom-call(f32[528,128]{1,0:T(8,128)} %pad.39.u0, f32[528,2112]{1,0:T(8,128)} %bitcast.23, f32[528,560]{1,0:T(8,128)} %get-tuple-element.11.amine, f32[528,560]{1,0:T(8,128)} %get-tuple-element.10.aother, f32[528,1120]{1,0:T(8,128)} %pad_maximum_fusion.bmat, f32[2,560,128]{2,1,0:T(8,128)} %pad.44.spec, ...), custom_call_target="tpu_custom_call" | custom-call | tf_op jit(solution)/shard_map/gmres/pallas_call | solution.py:424
  198.7 1.0 slice_bitcast_fusion
  199.7 0.2 copy.28
  199.9 0.1 reshape.102
  200.0 0.7 copy.29
  200.7 1.2 slice.79
  (61 shorter events, 2.1 us)
Async XLA Ops:
  6.6 2.1 %copy-start = (f32[528,1089]{1,0:T(8,128)S(1)}, f32[528,1089]{1,0:T(8,128)}, u32[]{:S(2)}) copy-start(f32[528,1089]{1,0:T(8,128)} %param.8) | copy-start | bytes 6899908
  6.6 2.1 %copy-start.3 = (pred[560]{0:T(1024)(128)(4,1)S(1)}, pred[560]{0:T(1024)(128)(4,1)}, u32[]{:S(2)}) copy-start(pred[560]{0:T(1024)(128)(4,1)} %constant.41.clone.1) | copy-start | bytes 1684
  10.5 1.9 copy-start.2
  12.7 1.3 copy-start.1
where the time goes:
time: 202 us
  Pallas kernels  184 us (91%)
  local copies, waits for them, and re-layouts  9.63 us (5%)
  other arithmetic  7.83 us (4%)
    pallas_call x1, Pallas kernels, per_device(): pl.pallas_call(functools.partial(kernel, groups, patches, lanes, blocks),...  184 us

commit v1 on v0

--- a/solution.py
+++ b/solution.py
@@ -31,6 +31,14 @@
 
 def dot(a, b):
     return jnp.dot(a, b, preferred_element_type=F32)
+
+
+def product(hi, lo, b):
+    rows = hi.shape[0]
+    cut = round_up(rows // 2, 16)
+    return jnp.concatenate(
+        [halves(dot(hi[a:z], b) + dot(lo[a:z], b)) for a, z in ((0, cut), (cut, rows))], 0
+    )
 
 
 def dot_nt(a, b):
@@ -79,7 +87,7 @@
 
 
 def pieces_of(rows):
-    return next(n for n in (1,) if rows // 8 % n == 0)
+    return next(n for n in (2, 1) if rows // 8 % n == 0)
 
 
 def tile_rows(total, unit, most):
@@ -94,13 +102,12 @@
     groups, patches, lanes, blocks,
     u0, kernel_t, amine, aother, bmat, spec, sel, mix,
     out, res,
-    image, packed, basis, vs, cs, pair, khi, klo, ahi, alo, bhi, blo, part_out, part_in, half_out, half_in,
+    raw, fresh, packed, basis, vs, cs, pair, khi, klo, ahi, alo, bhi, blo, part_out, part_in, half_out, half_in,
     sendrows, recvrows, msg1, msg2, hess, hrows,
     ag_send, ag_recv, fw_send, fw_recv, s1_send, s1_recv, s2_send, s2_recv, a2_send, a2_recv,
-    cf_send, cf_recv, sw_send, sw_recv,
+    cf_send, cf_recv, ex_send, ex_recv, sw_send, sw_recv,
 ):
     points = u0.shape[0]
-    total = basis.shape[1]
     half = spec.shape[1]
     main = packed.shape[2]
     pieces = pieces_of(main)
@@ -121,14 +128,12 @@
         pl.semaphore_signal(barrier, inc=1, device_id=(g, lax.rem(p + d, patches)), device_id_type=MESH)
 
     hess[...] = jnp.zeros_like(hess)
-    mine = pl.ds(pl.multiple_of(p * points, 8), points)
-
-    image[mine, :] = u0[...]
+    raw[0] = u0[...]
     pl.semaphore_wait(barrier, groups + patches - 2)
 
     swap = pltpu.make_async_remote_copy(
         src_ref=aother, dst_ref=pair.at[core],
-        send_sem=sw_send.at[1], recv_sem=sw_recv.at[1],
+        send_sem=sw_send.at[0], recv_sem=sw_recv.at[0],
         device_id=(g, sib), device_id_type=MESH,
     )
     swap.start()
@@ -142,46 +147,49 @@
 
     def dots(slot, count):
         def one(i, carry):
-            msg1[slot, p, pl.ds(i, 1), :] = jnp.sum(basis[i, mine, :] * image[mine, :], axis=0, keepdims=True)
+            msg1[slot, g, pl.ds(i, 1), :] = jnp.sum(basis[i] * raw[count], axis=0, keepdims=True)
             return carry
 
         lax.fori_loop(0, count, one, 0)
-        msg1[slot, p, ITERS : ITERS + 1, :] = jnp.sum(image[mine, :] * image[mine, :], axis=0, keepdims=True)
+        msg1[slot, g, ITERS : ITERS + 1, :] = jnp.sum(raw[count] * raw[count], axis=0, keepdims=True)
 
     def stage1(slot):
         return [
             pltpu.make_async_remote_copy(
-                src_ref=msg1.at[slot, p], dst_ref=msg1.at[slot, p],
+                src_ref=msg1.at[slot, g], dst_ref=msg1.at[slot, g],
                 send_sem=s1_send.at[slot, d], recv_sem=s1_recv.at[slot, d],
+                device_id=(lax.rem(g + d, groups), p), device_id_type=MESH,
+            )
+            for d in range(1, groups)
+        ]
+
+    def stage2(slot):
+        return [
+            pltpu.make_async_remote_copy(
+                src_ref=msg2.at[slot, p], dst_ref=msg2.at[slot, p],
+                send_sem=s2_send.at[slot, d], recv_sem=s2_recv.at[slot, d],
                 device_id=(g, lax.rem(p + d, patches)), device_id_type=MESH,
             )
             for d in range(1, patches)
         ]
 
-    def stage2(slot):
-        return [
-            pltpu.make_async_remote_copy(
-                src_ref=msg2.at[slot, g], dst_ref=msg2.at[slot, g],
-                send_sem=s2_send.at[slot, d], recv_sem=s2_recv.at[slot, d],
-                device_id=(lax.rem(g + d, groups), p), device_id_type=MESH,
-            )
-            for d in range(1, groups)
-        ]
-
-    def reduce_sums(slot, first):
+    def relay_sums(slot, first):
         for c in first:
             c.wait()
         local = msg1[slot, 0]
-        for q in range(1, patches):
+        for q in range(1, groups):
             local = local + msg1[slot, q]
-        msg2[slot, g] = local
+        msg2[slot, p] = local
         second = stage2(slot)
         for c in second:
             c.start()
+        return second
+
+    def finish_sums(slot, second):
         for c in second:
             c.wait()
         whole = msg2[slot, 0]
-        for q in range(1, groups):
+        for q in range(1, patches):
             whole = whole + msg2[slot, q]
         return jnp.sum(whole, axis=1, keepdims=True)
 
@@ -197,11 +205,11 @@
         hess[...] = jnp.where(lane_ids == lane, column, hess[...])
         return h, length
 
-    vrows = tile_rows(width, 16, 192)
+    vrows = tile_rows(points, 8, 96)
 
     def body(step, carry):
         slot = lax.rem(step, 2)
-        pack(packed.at[slot, p], image[mine, :], lanes)
+        pack(packed.at[slot, p], raw[step], lanes)
         own = pltpu.make_async_remote_copy(
             src_ref=packed.at[slot, p], dst_ref=packed.at[slot, p],
             send_sem=ag_send.at[slot, 0, 0], recv_sem=ag_recv.at[slot, 0, 0],
@@ -222,88 +230,76 @@
                     send_sem=fw_send.at[slot, k, n], recv_sem=fw_recv.at[slot, k, n],
                     device_id=(g, sib), device_id_type=MESH,
                 ))
+        for c in cross:
+            c.start()
+        own.start()
         dots(slot, step)
         first = stage1(slot)
         for c in first:
             c.start()
-        for c in cross:
-            c.start()
-        own.start()
-        h, length = record(step, reduce_sums(slot, first))
-        scale = jnp.broadcast_to(1.0 / length, (1, LANES))
-        hrows[...] = jnp.broadcast_to(h, (MSG, LANES))
-
-        def update(which):
-            @pl.loop(0, width // vrows)
-            def _(t):
-                at = pl.multiple_of(t * vrows, 16)
-                rows = pl.ds(pl.multiple_of(which * width + at, 16), vrows)
-                v = lax.fori_loop(
-                    0, step,
-                    lambda i, v: v - hrows[pl.ds(i, 1), :] * basis[i, rows, :],
-                    image[rows, :],
-                )
-                v = v * scale
-                basis[step, rows, :] = v
-                hi, lo = split(v)
-                vs[rows, :LANES] = hi
-                vs[rows, LANES:] = lo
+
+        def put(who, v):
+            rows = pl.ds(pl.multiple_of(who * points, 16), points)
+            hi, lo = split(v)
+            vs[rows, :LANES] = hi
+            vs[rows, LANES:] = lo
+
+        def place(who):
+            put(who, unpack(packed[slot, who], points, lanes))
 
         def wide(which):
             return vs[pl.ds(pl.multiple_of(which * width, 16), width), :]
 
-        def place(who):
-            rows = pl.ds(pl.multiple_of(who * points, 8), points)
-            image[rows, :] = unpack(packed[slot, who], points, lanes)
-
+        put(p, raw[step])
         own.wait()
         place(sib)
-        update(chip)
-        for c, f in zip(cross, forward):
-            c.wait()
-            f.start()
-        pack(part_out, halves(dot(ahi[...], wide(chip)) + dot(alo[...], wide(chip))), lanes)
+        near = wide(chip)
+        pack(part_out.at[slot], product(ahi, alo, near), lanes)
         partials = [
             pltpu.make_async_remote_copy(
-                src_ref=part_out, dst_ref=part_in.at[k - 1],
-                send_sem=cf_send.at[k], recv_sem=cf_recv.at[k],
+                src_ref=part_out.at[slot], dst_ref=part_in.at[slot, k - 1],
+                send_sem=cf_send.at[slot, k], recv_sem=cf_recv.at[slot, k],
                 device_id=(g, lax.rem(p + 2 * k, patches)), device_id_type=MESH,
             )
             for k in range(1, chips)
         ]
         for c in partials:
             c.start()
-        acc = dot(khi[chip], wide(chip)) + dot(klo[chip], wide(chip))
+        acc = product(khi.at[chip], klo.at[chip], near)
+        for c, f in zip(cross, forward):
+            c.wait()
+            f.start()
+        for k in range(1, chips):
+            place(lax.rem(p + patches - 2 * k, patches))
         for f in forward:
             f.wait()
         for k in range(1, chips):
             other = lax.rem(chip + chips - k, chips)
-            place(2 * other)
-            place(2 * other + 1)
-            update(other)
-            acc = acc + (dot(khi[other], wide(other)) + dot(klo[other], wide(other)))
-        whi, wlo = split(halves(acc))
-        sendrows[...] = dot_nt(sel[...], whi) + dot_nt(sel[...], wlo)
+            place(2 * other + 1 - core)
+            acc = acc + product(khi.at[other], klo.at[other], wide(other))
+        whi, wlo = split(acc)
+        sendrows[slot] = dot_nt(sel[...], whi) + dot_nt(sel[...], wlo)
         sends = []
         for d in sorted(range(1, groups), key=lambda d: min(d, groups - d) > 1):
             at, rows = blocks[d]
             sends.append(pltpu.make_async_remote_copy(
-                src_ref=sendrows.at[pl.ds(at, rows)], dst_ref=recvrows.at[pl.ds(at, rows)],
-                send_sem=a2_send.at[d], recv_sem=a2_recv.at[d],
+                src_ref=sendrows.at[slot, pl.ds(at, rows)], dst_ref=recvrows.at[slot, pl.ds(at, rows)],
+                send_sem=a2_send.at[slot, d], recv_sem=a2_recv.at[slot, d],
                 device_id=(lax.rem(g + d, groups), p), device_id_type=MESH,
             ))
         for c in sends:
             c.start()
-        recvrows[: blocks[0][1], :] = sendrows[: blocks[0][1], :]
-
-        coef = part_out[...]
+        second = relay_sums(slot, first)
+        recvrows[slot, : blocks[0][1], :] = sendrows[slot, : blocks[0][1], :]
+
+        coef = part_out[slot]
         for k, c in enumerate(partials, 1):
             c.wait()
-            coef = coef + part_in[k - 1]
-        half_out[...] = coef
+            coef = coef + part_in[slot, k - 1]
+        half_out[slot] = coef
         exchange = pltpu.make_async_remote_copy(
-            src_ref=half_out, dst_ref=half_in,
-            send_sem=sw_send.at[0], recv_sem=sw_recv.at[0],
+            src_ref=half_out.at[slot], dst_ref=half_in.at[slot],
+            send_sem=ex_send.at[slot], recv_sem=ex_recv.at[slot],
             device_id=(g, sib), device_id_type=MESH,
         )
         exchange.start()
@@ -312,17 +308,32 @@
             hi, lo = split(values)
             cs[:, :LANES] = hi
             cs[:, LANES:] = lo
-            return halves(dot(bhi[which], cs[...]) + dot(blo[which], cs[...]))
-
-        new = basis[step, mine, :] + self_half(core, unpack(coef, half, lanes) * spec[core])
+            return product(bhi.at[which], blo.at[which], cs[...])
+
+        fresh[...] = raw[step] + self_half(core, unpack(coef, half, lanes) * spec[core])
+        h, length = record(step, finish_sums(slot, second))
+        scale = jnp.broadcast_to(1.0 / length, (1, LANES))
+        hrows[...] = jnp.broadcast_to(h, (MSG, LANES))
+
+        @pl.loop(0, points // vrows)
+        def _(t):
+            rows = pl.ds(pl.multiple_of(t * vrows, 8), vrows)
+
+            def one(i, pair):
+                c = hrows[pl.ds(i, 1), :]
+                return pair[0] - c * basis[i, rows, :], pair[1] - c * raw[i + 1, rows, :]
+
+            v, z = lax.fori_loop(0, step, one, (raw[step, rows, :], fresh[rows, :]))
+            basis[step, rows, :] = v * scale
+            fresh[rows, :] = z
+
         exchange.wait()
-        new = new + self_half(1 - core, unpack(half_in[...], half, lanes) * spec[1 - core])
+        fresh[...] += self_half(1 - core, unpack(half_in[slot], half, lanes) * spec[1 - core])
+        mixes = jnp.concatenate(split(mix[...]), 1)
         for c in sends:
             c.wait()
-        rhi, rlo = split(recvrows[...])
-        mixes = jnp.concatenate(split(mix[...]), 1)
-        new = new + halves(dot_tn(rhi, mixes) + dot_tn(rlo, mixes))
-        image[mine, :] = new
+        rhi, rlo = split(recvrows[slot])
+        raw[step + 1] = (fresh[...] + halves(dot_tn(rhi, mixes) + dot_tn(rlo, mixes))) * scale
         return carry
 
     lax.fori_loop(0, ITERS, body, 0)
@@ -332,7 +343,7 @@
     first = stage1(slot)
     for c in first:
         c.start()
-    record(ITERS, reduce_sums(slot, first))
+    record(ITERS, finish_sums(slot, relay_sums(slot, first)))
 
     work = hess[...]
     beta = work[0:1, ITERS : ITERS + 1]
@@ -347,9 +358,9 @@
     for k in reversed(range(ITERS)):
         value = -jnp.sum(rows[k] * y, axis=1, keepdims=True)
         y = jnp.where(lane_ids == k, value, y)
-    answer = y[:, 0:1] * basis[0, mine, :]
+    answer = y[:, 0:1] * basis[0]
     for k in range(1, ITERS):
-        answer = answer + y[:, k : k + 1] * basis[k, mine, :]
+        answer = answer + y[:, k : k + 1] * basis[k]
     out[...] = answer
     left = work[:, ITERS : ITERS + 1]
     norm = jnp.sqrt(jnp.sum(left * left, axis=0, keepdims=True)) / beta
@@ -430,9 +441,10 @@
         in_specs=[vmem] * 8,
         out_specs=(vmem, vmem),
         scratch_shapes=[
-            pltpu.VMEM((total, LANES), F32),
+            pltpu.VMEM((ITERS + 1, points, LANES), F32),
+            pltpu.VMEM((points, LANES), F32),
             pltpu.VMEM((2, patches, main, LANES), F32),
-            pltpu.VMEM((ITERS, total, LANES), F32),
+            pltpu.VMEM((ITERS, points, LANES), F32),
             pltpu.VMEM((total, 2 * LANES), BF16),
             pltpu.VMEM((half, 2 * LANES), BF16),
             pltpu.VMEM((2, points, half), F32),
@@ -442,20 +454,20 @@
             pltpu.VMEM((half, 2 * points), BF16),
             pltpu.VMEM((2, points, half), BF16),
             pltpu.VMEM((2, points, half), BF16),
-            pltpu.VMEM((packed_rows(half), LANES), F32),
-            pltpu.VMEM((max(chips - 1, 1), packed_rows(half), LANES), F32),
-            pltpu.VMEM((packed_rows(half), LANES), F32),
-            pltpu.VMEM((packed_rows(half), LANES), F32),
-            pltpu.VMEM((total_rows, points), F32),
-            pltpu.VMEM((total_rows, points), F32),
+            pltpu.VMEM((2, packed_rows(half), LANES), F32),
+            pltpu.VMEM((2, max(chips - 1, 1), packed_rows(half), LANES), F32),
+            pltpu.VMEM((2, packed_rows(half), LANES), F32),
+            pltpu.VMEM((2, packed_rows(half), LANES), F32),
+            pltpu.VMEM((2, total_rows, points), F32),
+            pltpu.VMEM((2, total_rows, points), F32),
+            pltpu.VMEM((2, groups, MSG, LANES), F32),
             pltpu.VMEM((2, patches, MSG, LANES), F32),
-            pltpu.VMEM((2, groups, MSG, LANES), F32),
             pltpu.VMEM((MSG, LANES), F32),
             pltpu.VMEM((MSG, LANES), F32),
             dma((2, chips, pieces)), dma((2, chips, pieces)), dma((2, chips, pieces)), dma((2, chips, pieces)),
-            dma((2, patches)), dma((2, patches)), dma((2, groups)), dma((2, groups)),
-            dma((groups,)), dma((groups,)),
-            dma((chips,)), dma((chips,)), dma((2,)), dma((2,)),
+            dma((2, groups)), dma((2, groups)), dma((2, patches)), dma((2, patches)),
+            dma((2, groups)), dma((2, groups)),
+            dma((2, chips)), dma((2, chips)), dma((2,)), dma((2,)), dma((1,)), dma((1,)),
         ],
         compiler_params=pltpu.CompilerParams(
             collective_id=0, has_side_effects=True, vmem_limit_bytes=60 * 1024 * 1024

time: 202 us -> 174 us (0.86)
  Pallas kernels: 184 us -> 155 us
    pallas_call x1, Pallas kernels: 184 us -> 155 us  [per_device(): pl.pallas_call(functools.partial(kernel, groups, patches, lanes, blocks),...]
where the time goes in v1:
time: 174 us; the launch traced here: 173 us
  Pallas kernels  155 us (89%)
  local copies, waits for them, and re-layouts  9.63 us (6%)
  other arithmetic  7.83 us (4%)
    pallas_call x1, Pallas kernels, per_device(): pl.pallas_call(functools.partial(kernel, groups, patches, lanes, blocks),...  155 us

profile of v1, /device:TPU:0, one launch (start us, length us, event | category | flops | bytes accessed | tf_op | source)
XLA Modules:
  0.0 173.3 jit_solution(7180595610999285692)
XLA Ops:
  0.6 0.8 fusion.1
  2.0 0.8 fusion
  3.4 0.8 fusion.2
  4.7 0.1 tile.13
  5.1 0.7 and_select_fusion.mix
  5.8 0.7 and_convert_fusion.sel
  6.6 1.9 %slice.62 = f32[528,545]{1,0:T(8,128)S(1)} slice(f32[528,1089]{1,0:T(8,128)} %param.8), slice={[0:528], [544:1089]} | slice | bytes 2302080 | tf_op jit(solution)/shard_map/slice | solution.py:395
  8.5 0.2 copy-done
  8.6 1.9 %broadcast_select_fusion = (f32[528,560]{1,0:T(8,128)}, f32[528,560]{1,0:T(8,128)}, f32[528,560]{1,0:T(8,128)S(1)}, f32[528,560]{1,0:T(8,128)S(1)}) fusion(pred[]{:T(512)S(6)} %eq.22, f32[528,545]{1,0:T(8,128)S(1)} %slice.62, f32[528,1089]{1,0:T(8,128)S(1)} %copy-done, pred[560]{0:T(1024)(128)(4,1)S(1)} %copy-done.3), kind=kLoop, calls=%fused_computation.2 | loop fusion | flops 887040 | bytes 7065201 | tf_op jit(solution)/shard_map/jit(_where)/select_n | solution.py:401
  10.5 1.9 %pad_maximum_fusion.bmat = f32[528,1120]{1,0:T(8,128)} fusion(f32[528,560]{1,0:T(8,128)S(1)} %get-tuple-element.13, f32[528,560]{1,0:T(8,128)S(1)} %get-tuple-element.12), kind=kLoop, calls=%fused_computation | loop fusion | flops 591360 | bytes 4730880 | tf_op jit(solution)/shard_map/concatenate | solution.py:399
  12.5 0.1 copy.20
  12.7 0.1 broadcast_in_dim.22
  12.8 0.3 copy.21
  13.1 0.9 pad.44.spec
  13.9 0.2 copy.18
  14.1 0.1 reshape.91
  14.3 0.1 copy.19
  14.4 0.7 pad.39.u0
  15.1 155.1 %gmres.1 = (f32[528,128]{1,0:T(8,128)}, f32[8,128]{1,0:T(8,128)}) custom-call(f32[528,128]{1,0:T(8,128)} %pad.39.u0, f32[528,2112]{1,0:T(8,128)} %bitcast.23, f32[528,560]{1,0:T(8,128)} %get-tuple-element.11.amine, f32[528,560]{1,0:T(8,128)} %get-tuple-element.10.aother, f32[528,1120]{1,0:T(8,128)} %pad_maximum_fusion.bmat, f32[2,560,128]{2,1,0:T(8,128)} %pad.44.spec, ...), custom_call_target="tpu_custom_call" | custom-call | tf_op jit(solution)/shard_map/gmres/pallas_call | solution.py:435
  170.2 1.0 slice_bitcast_fusion
  171.2 0.2 copy.28
  171.3 0.1 reshape.102
  171.4 0.7 copy.29
  172.1 1.2 slice.79
  (61 shorter events, 2.1 us)
Async XLA Ops:
  6.6 2.1 %copy-start = (f32[528,1089]{1,0:T(8,128)S(1)}, f32[528,1089]{1,0:T(8,128)}, u32[]{:S(2)}) copy-start(f32[528,1089]{1,0:T(8,128)} %param.8) | copy-start | bytes 6899908
  6.6 2.1 %copy-start.3 = (pred[560]{0:T(1024)(128)(4,1)S(1)}, pred[560]{0:T(1024)(128)(4,1)}, u32[]{:S(2)}) copy-start(pred[560]{0:T(1024)(128)(4,1)} %constant.41.clone.1) | copy-start | bytes 1684
  10.5 1.9 %copy-start.2 = (f32[32,1089]{1,0:T(8,128)S(1)}, f32[32,1089]{1,0:T(8,128)}, u32[]{:S(2)}) copy-start(f32[32,1089]{1,0:T(8,128)} %param.9) | copy-start | bytes 418180
  12.7 1.3 copy-start.1

commit v2 on v1

--- a/solution.py
+++ b/solution.py
@@ -86,6 +86,10 @@
     return jnp.concatenate((jnp.where(lane < lanes, src, 0.0), end), 0)
 
 
+def low_modes(modes):
+    return max(modes // 2 // LANES * LANES, 0)
+
+
 def pieces_of(rows):
     return next(n for n in (2, 1) if rows // 8 % n == 0)
 
@@ -100,14 +104,19 @@
 
 def kernel(
     groups, patches, lanes, blocks,
-    u0, kernel_t, amine, aother, bmat, spec, sel, mix,
+    side, analysis, spectral, kernel_t, near_send, near_target, near_strength,
     out, res,
-    raw, fresh, packed, basis, vs, cs, pair, khi, klo, ahi, alo, bhi, blo, part_out, part_in, half_out, half_in,
+    raw, fresh, packed, basis, vs, cs, astage, kstage, both, pair, spec, sel, mixes,
+    khi, klo, ahi, alo, bhi, blo, part_out, part_in, half_out, half_in,
     sendrows, recvrows, msg1, msg2, hess, hrows,
     ag_send, ag_recv, fw_send, fw_recv, s1_send, s1_recv, s2_send, s2_recv, a2_send, a2_recv,
-    cf_send, cf_recv, ex_send, ex_recv, sw_send, sw_recv,
+    cf_send, cf_recv, ex_send, ex_recv, sw_send, sw_recv, in_sem,
 ):
-    points = u0.shape[0]
+    points = side.shape[1]
+    modes = analysis.shape[1]
+    cells = spectral.shape[0]
+    comps = lanes // cells
+    low = low_modes(modes)
     half = spec.shape[1]
     main = packed.shape[2]
     pieces = pieces_of(main)
@@ -120,6 +129,12 @@
     sib = p + 1 - 2 * core
     chips = patches // 2
 
+    loads = [
+        pltpu.make_async_copy(analysis, astage, in_sem.at[0]),
+        pltpu.make_async_copy(kernel_t, kstage, in_sem.at[1]),
+    ]
+    for c in loads:
+        c.start()
     msg1[...] = jnp.zeros_like(msg1)
     barrier = pltpu.get_barrier_semaphore()
     for d in range(1, groups):
@@ -128,22 +143,55 @@
         pl.semaphore_signal(barrier, inc=1, device_id=(g, lax.rem(p + d, patches)), device_id_type=MESH)
 
     hess[...] = jnp.zeros_like(hess)
-    raw[0] = u0[...]
+    pad = jnp.zeros((LANES - lanes, points), F32)
+    raw[0] = jnp.concatenate((side[...], pad), 0).T
     pl.semaphore_wait(barrier, groups + patches - 2)
 
-    swap = pltpu.make_async_remote_copy(
-        src_ref=aother, dst_ref=pair.at[core],
-        send_sem=sw_send.at[0], recv_sem=sw_recv.at[0],
-        device_id=(g, sib), device_id_type=MESH,
-    )
-    swap.start()
-    for c in range(chips):
-        khi[c], klo[c] = split(kernel_t[:, c * width : (c + 1) * width])
-    for c in range(2):
-        bhi[c], blo[c] = split(bmat[:, c * half : (c + 1) * half])
-    pair[core] = amine[...]
-    swap.wait()
-    ahi[...], alo[...] = split(pair[...].reshape(width, half).T)
+    def slot_rows(ref, who, rows, fill):
+        row = lax.broadcasted_iota(jnp.int32, (rows, ref.shape[1]), 0)
+        slot = lax.broadcasted_iota(jnp.int32, (rows, ref.shape[1]), 1)
+        count = rows // comps
+        hit = (row // comps == slot) & (row < count * comps)
+        values = jnp.broadcast_to(ref[pl.ds(who, 1), :].astype(F32), hit.shape)
+        found = jnp.sum(jnp.where(hit, values, 0.0), axis=1, keepdims=True)
+        return jnp.where(row[:, :1] < count * comps, found, fill)
+
+    def setup():
+        lane = lax.broadcasted_iota(jnp.int32, (1, LANES), 1)
+        cell = (lane % cells).astype(F32)
+        for d in range(groups):
+            at, rows = blocks[d]
+            row = lax.broadcasted_iota(jnp.int32, (rows, 1), 0)
+            same = (row % comps == lane // cells) & (lane < lanes)
+            ahead, behind = lax.rem(g + d, groups), lax.rem(g + groups - d, groups)
+            picks = same & (slot_rows(near_send, ahead, rows, -1.0) == cell)
+            sel[at : at + rows, :] = jnp.where(picks, 1.0, 0.0).astype(BF16)
+            hits = same & (slot_rows(near_target, behind, rows, -1.0) == cell)
+            mix = jnp.where(hits, slot_rows(near_strength, behind, rows, 0.0), 0.0)
+            mixes[at : at + rows, :LANES], mixes[at : at + rows, LANES:] = split(mix)
+        both[...] = jnp.zeros_like(both)
+        spec[...] = jnp.zeros_like(spec)
+        loads[0].wait()
+        both[0, :, :low] = astage[:, :low]
+        both[1, :, : modes - low] = astage[:, low:]
+        swap = pltpu.make_async_remote_copy(
+            src_ref=both.at[1 - core], dst_ref=pair.at[core],
+            send_sem=sw_send.at[0], recv_sem=sw_recv.at[0],
+            device_id=(g, sib), device_id_type=MESH,
+        )
+        swap.start()
+        each = spectral[...]
+        each = jnp.concatenate((each,) * comps + (jnp.zeros((LANES - lanes, modes), F32),), 0).T
+        spec[0, :low, :] = each[:low]
+        spec[1, : modes - low, :] = each[low:]
+        for c in range(2):
+            bhi[c], blo[c] = split(both[c])
+        loads[1].wait()
+        for c in range(chips):
+            khi[c], klo[c] = split(kstage[:, c * width : (c + 1) * width])
+        pair[core] = both[core]
+        swap.wait()
+        ahi[...], alo[...] = split(pair[...].reshape(width, half).T)
 
     def dots(slot, count):
         def one(i, carry):
@@ -237,6 +285,8 @@
         first = stage1(slot)
         for c in first:
             c.start()
+
+        pl.when(step == 0)(setup)
 
         def put(who, v):
             rows = pl.ds(pl.multiple_of(who * points, 16), points)
@@ -329,11 +379,10 @@
 
         exchange.wait()
         fresh[...] += self_half(1 - core, unpack(half_in[slot], half, lanes) * spec[1 - core])
-        mixes = jnp.concatenate(split(mix[...]), 1)
         for c in sends:
             c.wait()
         rhi, rlo = split(recvrows[slot])
-        raw[step + 1] = (fresh[...] + halves(dot_tn(rhi, mixes) + dot_tn(rlo, mixes))) * scale
+        raw[step + 1] = (fresh[...] + halves(dot_tn(rhi, mixes[...]) + dot_tn(rlo, mixes[...]))) * scale
         return carry
 
     lax.fori_loop(0, ITERS, body, 0)
@@ -361,7 +410,7 @@
     answer = y[:, 0:1] * basis[0]
     for k in range(1, ITERS):
         answer = answer + y[:, k : k + 1] * basis[k]
-    out[...] = answer
+    out[...] = answer.T[:lanes]
     left = work[:, ITERS : ITERS + 1]
     norm = jnp.sqrt(jnp.sum(left * left, axis=0, keepdims=True)) / beta
     res[...] = jnp.broadcast_to(norm, res.shape)
@@ -373,61 +422,13 @@
     modes = analysis.shape[1]
     lanes = cells * comps
     cap = near_send.shape[-1]
-    low = modes // 2
-    half = round_up(modes - low, 16)
-    pad = LANES - lanes
+    half = round_up(modes - low_modes(modes), 16)
     near_rows, far_rows = cap * comps, round_up(FAR_CAP * comps, 8)
     blocks, total_rows = blocks_of(groups, near_rows, far_rows)
-    g = lax.axis_index("cell")
-    core = lax.rem(lax.axis_index("patch"), 2)
-
-    u0 = jnp.pad(right_side.reshape(lanes, points).T, ((0, 0), (0, pad)))
-    kernel_t = near_kernel.T
-
-    def two_halves(x, axis):
-        def padded(piece):
-            pads = [(0, 0)] * x.ndim
-            pads[axis] = (0, half - piece.shape[axis])
-            return jnp.pad(piece, pads)
-
-        return (
-            padded(lax.slice_in_dim(x, 0, low, axis=axis)),
-            padded(lax.slice_in_dim(x, low, modes, axis=axis)),
-        )
-
-    first, second = two_halves(analysis, 1)
-    bmat = jnp.concatenate((first, second), 1)
-    amine = jnp.where(core == 0, first, second)
-    aother = jnp.where(core == 0, second, first)
-    spec_first, spec_second = two_halves(spectral, 1)
-    spec = jnp.stack((spec_first.T, spec_second.T))
-    spec = jnp.pad(jnp.repeat(spec, comps, axis=2), ((0, 0), (0, 0), (0, pad)))
-
-    def slot_rows(x, fill):
-        close = jnp.concatenate((x[:2], x[groups - 1 :]), 0)
-        far = x[2 : groups - 1, :FAR_CAP]
-        close = jnp.broadcast_to(close[:, :, None], close.shape + (comps,)).reshape(-1)
-        far = jnp.broadcast_to(far[:, :, None], far.shape + (comps,)).reshape(-1, FAR_CAP * comps)
-        far = jnp.pad(far, ((0, 0), (0, far_rows - FAR_CAP * comps)), constant_values=fill).reshape(-1)
-        return jnp.concatenate((close, far))[:, None]
-
-    def ahead(x):
-        return lax.dynamic_slice_in_dim(jnp.concatenate((x, x), 0), g, groups, 0)
-
-    def behind(x):
-        return lax.dynamic_slice_in_dim(jnp.concatenate((x, x), 0), g + 1, groups, 0)[::-1]
-
-    row_comp = jnp.concatenate((
-        jnp.tile(jnp.arange(comps), 3 * cap),
-        jnp.tile(jnp.pad(jnp.tile(jnp.arange(comps), FAR_CAP), (0, far_rows - FAR_CAP * comps), constant_values=-1), groups - 3),
-    ))[:, None]
-    lane = jnp.arange(LANES)[None, :]
-    same = (row_comp == lane % comps) & (lane < lanes)
-    sel = (same & (slot_rows(ahead(near_send[0]), -1) == lane // comps)).astype(BF16)
-    hit = same & (slot_rows(behind(near_target[0]), -1) == lane // comps)
-    mix = jnp.where(hit, slot_rows(behind(near_strength[0]), 0.0), 0.0)
+    side = right_side.transpose(1, 0, 2).reshape(lanes, points)
 
     vmem = pl.BlockSpec(memory_space=pltpu.VMEM)
+    hbm = pl.BlockSpec(memory_space=pl.ANY)
     dma = pltpu.SemaphoreType.DMA
     chips = max(patches // 2, 1)
     main = packed_rows(points)
@@ -435,10 +436,10 @@
     answer, residual = pl.pallas_call(
         functools.partial(kernel, groups, patches, lanes, blocks),
         out_shape=(
-            jax.ShapeDtypeStruct((points, LANES), F32),
+            jax.ShapeDtypeStruct((lanes, points), F32),
             jax.ShapeDtypeStruct((8, LANES), F32),
         ),
-        in_specs=[vmem] * 8,
+        in_specs=[vmem, hbm, vmem, hbm, vmem, vmem, vmem],
         out_specs=(vmem, vmem),
         scratch_shapes=[
             pltpu.VMEM((ITERS + 1, points, LANES), F32),
@@ -447,7 +448,13 @@
             pltpu.VMEM((ITERS, points, LANES), F32),
             pltpu.VMEM((total, 2 * LANES), BF16),
             pltpu.VMEM((half, 2 * LANES), BF16),
+            pltpu.VMEM((points, modes), F32),
+            pltpu.VMEM((points, total), F32),
             pltpu.VMEM((2, points, half), F32),
+            pltpu.VMEM((2, points, half), F32),
+            pltpu.VMEM((2, half, LANES), F32),
+            pltpu.VMEM((total_rows, LANES), BF16),
+            pltpu.VMEM((total_rows, 2 * LANES), BF16),
             pltpu.VMEM((chips, points, 2 * points), BF16),
             pltpu.VMEM((chips, points, 2 * points), BF16),
             pltpu.VMEM((half, 2 * points), BF16),
@@ -467,15 +474,14 @@
             dma((2, chips, pieces)), dma((2, chips, pieces)), dma((2, chips, pieces)), dma((2, chips, pieces)),
             dma((2, groups)), dma((2, groups)), dma((2, patches)), dma((2, patches)),
             dma((2, groups)), dma((2, groups)),
-            dma((2, chips)), dma((2, chips)), dma((2,)), dma((2,)), dma((1,)), dma((1,)),
+            dma((2, chips)), dma((2, chips)), dma((2,)), dma((2,)), dma((1,)), dma((1,)), dma((2,)),
         ],
         compiler_params=pltpu.CompilerParams(
             collective_id=0, has_side_effects=True, vmem_limit_bytes=60 * 1024 * 1024
         ),
         name="gmres",
-    )(u0, kernel_t, amine, aother, bmat, spec, sel, mix)
-    solution = answer[:, :lanes].T.reshape(cells, comps, points)
-    return solution, residual[0, 0]
+    )(side, analysis, spectral, near_kernel.T, near_send[0], near_target[0], near_strength[0])
+    return answer.reshape(comps, cells, points).transpose(1, 0, 2), residual[0, 0]
 
 
 def solution(mesh):

time: 174 us -> 151 us (0.87)
  Pallas kernels: 155 us -> 147 us
  other arithmetic: 7.83 us -> 0 us
  local copies, waits for them, and re-layouts: 9.63 us -> 2.84 us
    pallas_call x1, Pallas kernels: 155 us -> 147 us  [per_device(): pl.pallas_call(functools.partial(kernel, groups, patches, lanes, blocks),...]
    concatenate x10 -> x0, other arithmetic: 4.45 us -> none  [the longest x1 1.86 us: per_device(): bmat = jnp.concatenate((first, second), 1)]
    select_n x3 -> x0, other arithmetic: 2.64 us -> none  [the longest x1 1.89 us: per_device(): aother = jnp.where(core == 0, second, first)]
    slice x19 -> x1, local copies, waits for them, and re-layouts: 3.57 us -> 1.19 us  [per_device(): residual[0, 0]]
where the time goes in v2:
time: 151 us
  Pallas kernels  147 us (97%)
  local copies, waits for them, and re-layouts  2.84 us (2%)
    pallas_call x1, Pallas kernels, per_device(): pl.pallas_call(functools.partial(kernel, groups, patches, lanes, blocks),...  147 us

profile of v2, /device:TPU:0, one launch (start us, length us, event | category | flops | bytes accessed | tf_op | source)
XLA Modules:
  0.0 150.7 jit_solution(4627839584701757366)
XLA Ops:
  0.6 147.2 %gmres.1 = (f32[96,528]{1,0:T(8,128)}, f32[8,128]{1,0:T(8,128)}) custom-call(f32[96,528]{1,0:T(8,128)} %bitcast.12, f32[528,1089]{1,0:T(8,128)} %analysis.1, f32[32,1089]{1,0:T(8,128)} %spectral.1, f32[528,2112]{1,0:T(8,128)} %bitcast.11, s32[8,8]{1,0:T(8,128)} %bitcast.14, s32[8,8]{1,0:T(8,128)} %bitcast.15, f32[8,8]{1,0:T(8,128)} %bitcast.16), custom_call_target="tpu_custom_call" | custom-call | tf_op jit(solution)/shard_map/gmres/pallas_call | solution.py:436
  147.9 1.2 slice.3
  149.0 1.7 %copy.10 = f32[32,3,528]{2,0,1:T(8,128)} copy(f32[32,3,528]{2,0,1:T(8,128)} %bitcast.13) | data formatting | bytes 405504

commit v3 on v2

--- a/solution.py
+++ b/solution.py
@@ -90,8 +90,18 @@
     return max(modes // 2 // LANES * LANES, 0)
 
 
-def pieces_of(rows):
-    return next(n for n in (2, 1) if rows // 8 % n == 0)
+def cuts_of(points):
+    cut = points // 2 // LANES * LANES
+    return ((0, cut), (cut, points)) if cut else ((0, points),)
+
+
+def spans_of(points):
+    spans, at = [], 0
+    for a, z in cuts_of(points):
+        rows = packed_rows(z - a)
+        spans.append((at, rows))
+        at += rows
+    return spans, at
 
 
 def tile_rows(total, unit, most):
@@ -118,9 +128,9 @@
     comps = lanes // cells
     low = low_modes(modes)
     half = spec.shape[1]
-    main = packed.shape[2]
-    pieces = pieces_of(main)
-    chunk = main // pieces
+    cuts = cuts_of(points)
+    spans, _ = spans_of(points)
+    pieces = len(cuts)
     width = 2 * points
     g = lax.axis_index("cell")
     p = lax.axis_index("patch")
@@ -188,10 +198,16 @@
             bhi[c], blo[c] = split(both[c])
         loads[1].wait()
         for c in range(chips):
-            khi[c], klo[c] = split(kstage[:, c * width : (c + 1) * width])
+            for a, z in cuts:
+                one = kstage[:, c * width + a : c * width + z]
+                two = kstage[:, c * width + points + a : c * width + points + z]
+                for i, x in enumerate((jnp.where(core == 0, one, two), jnp.where(core == 0, two, one))):
+                    at = 2 * a + i * (z - a)
+                    khi[c, :, at : at + z - a], klo[c, :, at : at + z - a] = split(x)
         pair[core] = both[core]
         swap.wait()
-        ahi[...], alo[...] = split(pair[...].reshape(width, half).T)
+        parts = [pair[who, a:z] for a, z in cuts for who in (core, 1 - core)]
+        ahi[...], alo[...] = split(jnp.concatenate(parts, 0).T)
 
     def dots(slot, count):
         def one(i, carry):
@@ -257,7 +273,8 @@
 
     def body(step, carry):
         slot = lax.rem(step, 2)
-        pack(packed.at[slot, p], raw[step], lanes)
+        for (a, z), (at, rows) in zip(cuts, spans):
+            pack(packed.at[slot, p, pl.ds(at, rows)], raw[step, a:z], lanes)
         own = pltpu.make_async_remote_copy(
             src_ref=packed.at[slot, p], dst_ref=packed.at[slot, p],
             send_sem=ag_send.at[slot, 0, 0], recv_sem=ag_recv.at[slot, 0, 0],
@@ -265,7 +282,7 @@
         )
         cross, forward = [], []
         for n in range(pieces):
-            rows = pl.ds(n * chunk, chunk)
+            rows = pl.ds(*spans[n])
             for k in range(1, chips):
                 cross.append(pltpu.make_async_remote_copy(
                     src_ref=packed.at[slot, p, rows], dst_ref=packed.at[slot, p, rows],
@@ -288,22 +305,24 @@
 
         pl.when(step == 0)(setup)
 
-        def put(who, v):
-            rows = pl.ds(pl.multiple_of(who * points, 16), points)
+        def put(which, n, i, v):
+            a, z = cuts[n]
+            rows = slice(2 * a + i * (z - a), 2 * a + (i + 1) * (z - a))
             hi, lo = split(v)
-            vs[rows, :LANES] = hi
-            vs[rows, LANES:] = lo
-
-        def place(who):
-            put(who, unpack(packed[slot, who], points, lanes))
-
-        def wide(which):
-            return vs[pl.ds(pl.multiple_of(which * width, 16), width), :]
-
-        put(p, raw[step])
+            vs[which, rows, :LANES] = hi
+            vs[which, rows, LANES:] = lo
+
+        def place(which, n, i):
+            who = 2 * which + (core if i == 0 else 1 - core)
+            at, rows = spans[n]
+            put(which, n, i, unpack(packed[slot, who, at : at + rows], cuts[n][1] - cuts[n][0], lanes))
+
+        for n, (a, z) in enumerate(cuts):
+            put(chip, n, 0, raw[step, a:z])
         own.wait()
-        place(sib)
-        near = wide(chip)
+        for n in range(pieces):
+            place(chip, n, 1)
+        near = vs[chip]
         pack(part_out.at[slot], product(ahi, alo, near), lanes)
         partials = [
             pltpu.make_async_remote_copy(
@@ -316,17 +335,18 @@
         for c in partials:
             c.start()
         acc = product(khi.at[chip], klo.at[chip], near)
-        for c, f in zip(cross, forward):
-            c.wait()
-            f.start()
-        for k in range(1, chips):
-            place(lax.rem(p + patches - 2 * k, patches))
-        for f in forward:
-            f.wait()
-        for k in range(1, chips):
-            other = lax.rem(chip + chips - k, chips)
-            place(2 * other + 1 - core)
-            acc = acc + product(khi.at[other], klo.at[other], wide(other))
+        for n in range(pieces):
+            a, z = 2 * cuts[n][0], 2 * cuts[n][1]
+            here = [(k, cross[n * (chips - 1) + k - 1], forward[n * (chips - 1) + k - 1]) for k in range(1, chips)]
+            for k, c, f in here:
+                c.wait()
+                f.start()
+                place(lax.rem(chip + chips - k, chips), n, 0)
+            for k, c, f in here:
+                other = lax.rem(chip + chips - k, chips)
+                f.wait()
+                place(other, n, 1)
+                acc = acc + product(khi.at[other, :, a:z], klo.at[other, :, a:z], vs[other, a:z])
         whi, wlo = split(acc)
         sendrows[slot] = dot_nt(sel[...], whi) + dot_nt(sel[...], wlo)
         sends = []
@@ -431,8 +451,8 @@
     hbm = pl.BlockSpec(memory_space=pl.ANY)
     dma = pltpu.SemaphoreType.DMA
     chips = max(patches // 2, 1)
-    main = packed_rows(points)
-    pieces = pieces_of(main)
+    pieces = len(cuts_of(points))
+    _, main = spans_of(points)
     answer, residual = pl.pallas_call(
         functools.partial(kernel, groups, patches, lanes, blocks),
         out_shape=(
@@ -446,7 +466,7 @@
             pltpu.VMEM((points, LANES), F32),
             pltpu.VMEM((2, patches, main, LANES), F32),
             pltpu.VMEM((ITERS, points, LANES), F32),
-            pltpu.VMEM((total, 2 * LANES), BF16),
+            pltpu.VMEM((chips, 2 * points, 2 * LANES), BF16),
             pltpu.VMEM((half, 2 * LANES), BF16),
             pltpu.VMEM((points, modes), F32),
             pltpu.VMEM((points, total), F32),

time: 151 us -> 150 us (level)
  no operation moved by 1% of the time
where the time goes in v3:
time: 150 us
  Pallas kernels  147 us (98%)
  local copies, waits for them, and re-layouts  2.84 us (2%)
    pallas_call x1, Pallas kernels, per_device(): pl.pallas_call(functools.partial(kernel, groups, patches, lanes, blocks),...  147 us

profile of v3, /device:TPU:0, one launch (start us, length us, event | category | flops | bytes accessed | tf_op | source)
XLA Modules:
  0.0 150.1 jit_solution(8388253700637718361)
XLA Ops:
  0.6 146.6 %gmres.1 = (f32[96,528]{1,0:T(8,128)}, f32[8,128]{1,0:T(8,128)}) custom-call(f32[96,528]{1,0:T(8,128)} %bitcast.12, f32[528,1089]{1,0:T(8,128)} %analysis.1, f32[32,1089]{1,0:T(8,128)} %spectral.1, f32[528,2112]{1,0:T(8,128)} %bitcast.11, s32[8,8]{1,0:T(8,128)} %bitcast.14, s32[8,8]{1,0:T(8,128)} %bitcast.15, f32[8,8]{1,0:T(8,128)} %bitcast.16), custom_call_target="tpu_custom_call" | custom-call | tf_op jit(solution)/shard_map/gmres/pallas_call | solution.py:456
  147.3 1.2 slice.3
  148.5 1.7 %copy.10 = f32[32,3,528]{2,0,1:T(8,128)} copy(f32[32,3,528]{2,0,1:T(8,128)} %bitcast.13) | data formatting | bytes 405504

commit v4 on v3

--- a/solution.py
+++ b/solution.py
@@ -90,6 +90,16 @@
     return max(modes // 2 // LANES * LANES, 0)
 
 
+def tiles_of(blocks, points):
+    most = max(rows for _, rows in blocks.values())
+    tiles, at = {}, 0
+    for d, (_, rows) in blocks.items():
+        count = rows // 8 * (points // LANES) + (rows == most)
+        tiles[d] = (at, count)
+        at += count
+    return tiles, at
+
+
 def cuts_of(points):
     cut = points // 2 // LANES * LANES
     return ((0, cut), (cut, points)) if cut else ((0, points),)
@@ -118,7 +128,7 @@
     out, res,
     raw, fresh, packed, basis, vs, cs, astage, kstage, both, pair, spec, sel, mixes,
     khi, klo, ahi, alo, bhi, blo, part_out, part_in, half_out, half_in,
-    sendrows, recvrows, msg1, msg2, hess, hrows,
+    sendt, recvt, recvrows, msg1, msg2, hess, hrows,
     ag_send, ag_recv, fw_send, fw_recv, s1_send, s1_recv, s2_send, s2_recv, a2_send, a2_recv,
     cf_send, cf_recv, ex_send, ex_recv, sw_send, sw_recv, in_sem,
 ):
@@ -270,6 +280,12 @@
         return h, length
 
     vrows = tile_rows(points, 8, 96)
+    base = points // LANES * LANES
+    tail = points - base
+    wide_tiles = base // LANES
+    tiles, _ = tiles_of(blocks, points)
+    row8 = lax.broadcasted_iota(jnp.int32, (8, LANES), 0)
+    keep = lax.broadcasted_iota(jnp.int32, (8, LANES), 1) // tail == row8
 
     def body(step, carry):
         slot = lax.rem(step, 2)
@@ -347,20 +363,39 @@
                 f.wait()
                 place(other, n, 1)
                 acc = acc + product(khi.at[other, :, a:z], klo.at[other, :, a:z], vs[other, a:z])
-        whi, wlo = split(acc)
-        sendrows[slot] = dot_nt(sel[...], whi) + dot_nt(sel[...], wlo)
+        whi, wlo = split(jnp.concatenate((acc[:base],) + (acc[base:],) * (LANES // tail), 0))
+        picked = dot_nt(sel[...], whi) + dot_nt(sel[...], wlo)
+        ends = [
+            jnp.sum(jnp.where(keep, picked[r : r + 8, base:], 0.0), axis=0, keepdims=True)
+            for r in range(0, picked.shape[0], 8)
+        ]
+        for d in range(groups):
+            at, rows = blocks[d]
+            first_tile, count = tiles[d]
+            for i in range(rows // 8):
+                for c in range(wide_tiles):
+                    v = picked[at + 8 * i : at + 8 * i + 8, c * LANES : (c + 1) * LANES]
+                    if c == 0 and count == wide_tiles:
+                        v = jnp.where(row8 == 7, ends[at // 8], v)
+                    sendt[slot, first_tile + i * wide_tiles + c] = v
+            if count > rows // 8 * wide_tiles:
+                extra = jnp.zeros((8, LANES), F32)
+                for i in range(rows // 8):
+                    extra = jnp.where(row8 == i, ends[at // 8 + i], extra)
+                sendt[slot, first_tile + count - 1] = extra
         sends = []
         for d in sorted(range(1, groups), key=lambda d: min(d, groups - d) > 1):
-            at, rows = blocks[d]
+            part = pl.ds(*tiles[d])
             sends.append(pltpu.make_async_remote_copy(
-                src_ref=sendrows.at[slot, pl.ds(at, rows)], dst_ref=recvrows.at[slot, pl.ds(at, rows)],
+                src_ref=sendt.at[slot, part], dst_ref=recvt.at[slot, part],
                 send_sem=a2_send.at[slot, d], recv_sem=a2_recv.at[slot, d],
                 device_id=(lax.rem(g + d, groups), p), device_id_type=MESH,
             ))
         for c in sends:
             c.start()
         second = relay_sums(slot, first)
-        recvrows[slot, : blocks[0][1], :] = sendrows[slot, : blocks[0][1], :]
+        own_tiles = slice(tiles[0][0], tiles[0][0] + tiles[0][1])
+        recvt[slot, own_tiles] = sendt[slot, own_tiles]
 
         coef = part_out[slot]
         for k, c in enumerate(partials, 1):
@@ -401,8 +436,25 @@
         fresh[...] += self_half(1 - core, unpack(half_in[slot], half, lanes) * spec[1 - core])
         for c in sends:
             c.wait()
-        rhi, rlo = split(recvrows[slot])
-        raw[step + 1] = (fresh[...] + halves(dot_tn(rhi, mixes[...]) + dot_tn(rlo, mixes[...]))) * scale
+        for d in range(groups):
+            at, rows = blocks[d]
+            first_tile, count = tiles[d]
+            for i in range(rows // 8):
+                here = slice(at + 8 * i, at + 8 * i + 8)
+                for c in range(wide_tiles):
+                    recvrows[here, c * LANES : (c + 1) * LANES] = recvt[slot, first_tile + i * wide_tiles + c]
+                if count == wide_tiles:
+                    end = recvt[slot, first_tile, 7:8, :]
+                else:
+                    end = recvt[slot, first_tile + count - 1, i : i + 1, :]
+                recvrows[here, base:] = jnp.where(keep, jnp.broadcast_to(end, (8, LANES)), 0.0)
+        rhi, rlo = split(recvrows[...])
+        added = halves(dot_tn(rhi, mixes[...]) + dot_tn(rlo, mixes[...]))
+        last = added[base : base + tail]
+        for k in range(1, LANES // tail):
+            last = last + added[base + k * tail : base + (k + 1) * tail]
+        raw[step + 1, :base] = (fresh[:base] + added[:base]) * scale
+        raw[step + 1, base:] = (fresh[base:] + last) * scale
         return carry
 
     lax.fori_loop(0, ITERS, body, 0)
@@ -445,6 +497,7 @@
     half = round_up(modes - low_modes(modes), 16)
     near_rows, far_rows = cap * comps, round_up(FAR_CAP * comps, 8)
     blocks, total_rows = blocks_of(groups, near_rows, far_rows)
+    _, tile_count = tiles_of(blocks, points)
     side = right_side.transpose(1, 0, 2).reshape(lanes, points)
 
     vmem = pl.BlockSpec(memory_space=pltpu.VMEM)
@@ -485,8 +538,9 @@
             pltpu.VMEM((2, max(chips - 1, 1), packed_rows(half), LANES), F32),
             pltpu.VMEM((2, packed_rows(half), LANES), F32),
             pltpu.VMEM((2, packed_rows(half), LANES), F32),
-            pltpu.VMEM((2, total_rows, points), F32),
-            pltpu.VMEM((2, total_rows, points), F32),
+            pltpu.VMEM((2, tile_count, 8, LANES), F32),
+            pltpu.VMEM((2, tile_count, 8, LANES), F32),
+            pltpu.VMEM((total_rows, round_up(points, LANES)), F32),
             pltpu.VMEM((2, groups, MSG, LANES), F32),
             pltpu.VMEM((2, patches, MSG, LANES), F32),
             pltpu.VMEM((MSG, LANES), F32),

time: 150 us -> 146 us (0.973)
  Pallas kernels: 147 us -> 142 us
    pallas_call x1, Pallas kernels: 147 us -> 142 us  [per_device(): pl.pallas_call(functools.partial(kernel, groups, patches, lanes, blocks),...]
where the time goes in v4:
time: 146 us
  Pallas kernels  142 us (97%)
  local copies, waits for them, and re-layouts  2.84 us (2%)
    pallas_call x1, Pallas kernels, per_device(): pl.pallas_call(functools.partial(kernel, groups, patches, lanes, blocks),...  142 us

profile of v4, /device:TPU:0, one launch (start us, length us, event | category | flops | bytes accessed | tf_op | source)
XLA Modules:
  0.0 145.7 jit_solution(2620827147249354175)
XLA Ops:
  0.6 142.2 %gmres.1 = (f32[96,528]{1,0:T(8,128)}, f32[8,128]{1,0:T(8,128)}) custom-call(f32[96,528]{1,0:T(8,128)} %bitcast.12, f32[528,1089]{1,0:T(8,128)} %analysis.1, f32[32,1089]{1,0:T(8,128)} %spectral.1, f32[528,2112]{1,0:T(8,128)} %bitcast.11, s32[8,8]{1,0:T(8,128)} %bitcast.14, s32[8,8]{1,0:T(8,128)} %bitcast.15, f32[8,8]{1,0:T(8,128)} %bitcast.16), custom_call_target="tpu_custom_call" | custom-call | tf_op jit(solution)/shard_map/gmres/pallas_call | solution.py:509
  142.8 1.2 slice.3
  144.0 1.7 %copy.10 = f32[32,3,528]{2,0,1:T(8,128)} copy(f32[32,3,528]{2,0,1:T(8,128)} %bitcast.13) | data formatting | bytes 405504
